TPU v7x, 32 devices: a whole 2x2x4 slice. The times are simulated.
32 devices in a mesh: groups: 2 (over y), row: 4 (over x, core), col: 4 (over z).
Axes of the slice: x: 2, y: 2, z: 4, core: 2. Of those that a mesh axis runs over, the one named last changes fastest.
Arguments:
- inputs: bfloat16 [1536, 4096], P(('groups', 'col'), 'row'), parts along dimension 0, may hold values from -6 to 6
- cotangent: bfloat16 [1536, 4096], P(('groups', 'col'), 'row'), parts along dimension 0, may hold values from -6 to 6
- preactivation: bfloat16 [1536, 8192], P(('groups', 'row'), 'col'), parts along dimension 0, may hold values from -8 to 8
- up_weight: bfloat16 [4096, 8192], P('row', 'col'), may hold values from -0.09375 to 0.09375
- down_weight: bfloat16 [8192, 4096], P('col', 'row'), may hold values from -0.0625 to 0.0625
Outputs:
- grad_input: bfloat16 [1536, 4096], P(('groups', 'col'), 'row'), parts along dimension 0
- grad_up: float32 [8192, 8192], P(('groups', 'row'), 'col'), parts along dimension 0
- grad_down: float32 [16384, 4096], P(('groups', 'col'), 'row'), parts along dimension 0
There are 2 independent parts, one for each index of `groups`. A program takes and returns all parts, laid end to end along the dimension named above; an argument that names none is the same for every part. Nothing has to cross between parts.
All inputs are finite; a program needn't handle non-finite values.
Results may differ from a plain program's by a relative error of at most 0.0049.
Values may be sent and summed in bfloat16 or wider, within the bound.
A program may use at most 128 MiB of HBM per device.

v0:
```python
import math

import jax
import jax.numpy as jnp
from jax import lax
from jax.sharding import PartitionSpec as P


def gelu_pair(values):
    v = values.astype(jnp.float32)
    tanh_arg = 0.7978845608 * (v + 0.044715 * v * v * v)
    tanh_val = jnp.tanh(tanh_arg)
    gelu_value = 0.5 * v * (1.0 + tanh_val)
    gelu_slope = 0.5 * (1.0 + tanh_val) + 0.5 * v * (1.0 - tanh_val * tanh_val) * 0.7978845608 * (
        1.0 + 3.0 * 0.044715 * v * v
    )
    return (gelu_value, gelu_slope)


def per_device(inputs, cotangent, preactivation, up_weight, down_weight):
    inputs_all, cotangent_all = (
        lax.all_gather(inputs, "col", axis=0, tiled=True),
        lax.all_gather(cotangent, "col", axis=0, tiled=True),
    )
    total_tokens = inputs_all.shape[0]
    token_scale = 1.0 / math.sqrt(total_tokens)
    last_dims = (((1,), (1,)), ((), ()))
    first_dims = (((0,), (0,)), ((), ()))
    piece = cotangent_all
    hidden_grad = lax.psum_scatter(
        lax.dot_general(piece, down_weight, last_dims, preferred_element_type=jnp.float32),
        "row",
        scatter_dimension=0,
        tiled=True,
    )
    gelu_value, gelu_slope = gelu_pair(preactivation)
    activation = gelu_value.astype(jnp.bfloat16)
    pre_grad = (hidden_grad * gelu_slope).astype(jnp.bfloat16)
    activation_all, pre_grad_all = (
        lax.all_gather(activation, "row", axis=0, tiled=True),
        lax.all_gather(pre_grad, "row", axis=0, tiled=True),
    )
    piece = pre_grad_all
    grad_input = lax.psum_scatter(
        lax.dot_general(piece, up_weight, last_dims, preferred_element_type=jnp.float32),
        "col",
        scatter_dimension=0,
        tiled=True,
    ).astype(jnp.bfloat16)
    grad_up = (
        lax.dot_general(inputs_all, pre_grad_all, first_dims, preferred_element_type=jnp.float32)
        * token_scale
    )
    grad_down = (
        lax.dot_general(
            activation_all, cotangent_all, first_dims, preferred_element_type=jnp.float32
        )
        * token_scale
    )
    return (grad_input, grad_up, grad_down)


def solution(mesh):
    placed = (
        P(("groups", "col"), "row"),
        P(("groups", "col"), "row"),
        P(("groups", "row"), "col"),
        P("row", "col"),
        P("col", "row"),
    )
    return jax.shard_map(
        per_device,
        mesh=mesh,
        in_specs=placed,
        out_specs=(
            P(("groups", "col"), "row"),
            P(("groups", "row"), "col"),
            P(("groups", "col"), "row"),
        ),
        check_vma=False,
    )
```

profile of v0, /device:TPU:0, one launch (start us, length us, event | category | flops | bytes accessed | tf_op | source)
XLA Modules:
  0.0 287.1 jit_solution(9059382792913873849)
XLA Ops:
  7.2 0.0 all-gather.5.cloned.1.call-start
  7.2 0.7 all-gather.5.cloned.1.call-update
  7.9 0.0 reduce-scatter.3.cloned.1.call-start
  7.9 41.4 %all-gather.5.cloned.1.call-done = bf16[768,1024]{1,0:T(8,128)(2,1)} async-done(((bf16[192,1024]{1,0:T(8,128)(2,1)}), bf16[768,1024]{1,0:T(8,128)(2,1)}) %all-gather.5.cloned.1.call-update) | async-done | bytes 1572880 | tf_op jit(solution)/shard_map/all_gather | solution.py:23
  49.3 8.8 %fusion.11 = f32[768,2048]{1,0:T(8,128)} fusion(bf16[768,1024]{1,0:T(8,128)(2,1)} %all-gather.5.cloned.1.call-done, bf16[2048,1024]{1,0:T(8,128)(2,1)} %param.9), kind=kOutput, calls=%fused_computation.20 | convolution fusion | flops 3221225472 | bytes 12058624 | tf_op jit(solution)/shard_map/dot_general | solution.py:31
  58.1 0.0 copy-start
  58.1 0.0 reduce-scatter.3.cloned.1.call-update
  58.2 0.0 all-gather.7.cloned.1.call-start
  58.2 57.8 %reduce-scatter.3.cloned.1.call-done = f32[192,2048]{1,0:T(8,128)} async-done(((f32[768,2048]{1,0:T(8,128)}), f32[192,2048]{1,0:T(8,128)}) %reduce-scatter.3.cloned.1.call-update) | async-done | bytes 1572880 | tf_op jit(solution)/shard_map/reduce_scatter | solution.py:30
  116.0 0.0 copy-done
  116.0 3.7 %fusion.7 = (bf16[192,2048]{1,0:T(8,128)(2,1)}, bf16[192,2048]{1,0:T(8,128)(2,1)}) fusion(bf16[192,2048]{1,0:T(8,128)(2,1)S(1)} %copy-done, f32[192,2048]{1,0:T(8,128)} %reduce-scatter.3.cloned.1.call-done), kind=kLoop, calls=%fused_computation.16 | loop fusion | flops 8650752 | bytes 3932160 | tf_op jit(solution)/shard_map/convert_element_type | solution.py:37
  119.7 0.0 all-gather.7.cloned.1.call-update
  119.7 0.0 all-gather.9.cloned.1.call-start
  119.8 0.5 all-gather.9.cloned.1.call-update
  120.3 0.0 all-gather.11.cloned.1.call-start
  120.4 0.5 all-gather.11.cloned.1.call-update
  120.9 0.0 reduce-scatter.5.cloned.1.call-start
  121.0 27.4 %all-gather.7.cloned.1.call-done = bf16[768,2048]{1,0:T(8,128)(2,1)} async-done(((bf16[192,2048]{1,0:T(8,128)(2,1)}), bf16[768,2048]{1,0:T(8,128)(2,1)}) %all-gather.7.cloned.1.call-update) | async-done | bytes 3145744 | tf_op jit(solution)/shard_map/all_gather | solution.py:41
  148.4 8.3 %fusion.12 = f32[768,1024]{1,0:T(8,128)} fusion(bf16[768,2048]{1,0:T(8,128)(2,1)} %all-gather.7.cloned.1.call-done, bf16[1024,2048]{1,0:T(8,128)(2,1)} %param.8), kind=kOutput, calls=%fused_computation.21 | convolution fusion | flops 3221225472 | bytes 10485760 | tf_op jit(solution)/shard_map/dot_general | solution.py:45
  156.7 0.0 copy-start.1
  156.7 0.0 reduce-scatter.5.cloned.1.call-update
  156.7 30.2 %all-gather.9.cloned.1.call-done = bf16[768,1024]{1,0:T(8,128)(2,1)} async-done(((bf16[192,1024]{1,0:T(8,128)(2,1)}), bf16[768,1024]{1,0:T(8,128)(2,1)}) %all-gather.9.cloned.1.call-update) | async-done | bytes 1572880 | tf_op jit(solution)/shard_map/all_gather | solution.py:22
  186.9 0.0 copy-done.1
  186.9 7.1 %multiply_bitcast_fusion = f32[1024,2048]{0,1:T(8,128)} fusion(bf16[768,2048]{1,0:T(8,128)(2,1)S(1)} %copy-done.1, bf16[768,1024]{1,0:T(8,128)(2,1)} %all-gather.9.cloned.1.call-done), kind=kOutput, calls=%fused_computation | convolution fusion | flops 3223322624 | bytes 13107200 | tf_op jit(solution)/shard_map/dot_general | solution.py:51
  194.0 0.0 copy-start.2
  194.0 9.4 %copy.8 = f32[1024,2048]{1,0:T(8,128)} copy(f32[1024,2048]{0,1:T(8,128)} %multiply_bitcast_fusion) | data formatting | bytes 16777216
  203.4 12.3 %all-gather.11.cloned.1.call-done = bf16[768,2048]{1,0:T(8,128)(2,1)} async-done(((bf16[192,2048]{1,0:T(8,128)(2,1)}), bf16[768,2048]{1,0:T(8,128)(2,1)}) %all-gather.11.cloned.1.call-update) | async-done | bytes 3145744 | tf_op jit(solution)/shard_map/all_gather | solution.py:40
  215.7 0.0 copy-done.2
  215.7 7.6 %convolution_multiply_fusion = f32[2048,1024]{1,0:T(8,128)} fusion(bf16[768,2048]{1,0:T(8,128)(2,1)} %all-gather.11.cloned.1.call-done, bf16[768,1024]{1,0:T(8,128)(2,1)S(1)} %copy-done.2), kind=kOutput, calls=%fused_computation.1 | convolution fusion | flops 3223322624 | bytes 13107200 | tf_op jit(solution)/shard_map/dot_general | solution.py:55
  223.3 55.0 %reduce-scatter.5.cloned.1.call-done = f32[192,1024]{1,0:T(8,128)} async-done(((f32[768,1024]{1,0:T(8,128)}), f32[192,1024]{1,0:T(8,128)}) %reduce-scatter.5.cloned.1.call-update) | async-done | bytes 786448 | tf_op jit(solution)/shard_map/reduce_scatter | solution.py:44
  278.3 1.9 convert_element_type.14
Async XLA Ops:
  7.2 42.2 %all-gather.5.cloned.1.call-start = ((), (), s32[]{:S(2)}) async-start(), calls=%async_computation.2 | async-start | bytes 1966080 | tf_op jit(solution)/shard_map/all_gather | solution.py:23
  7.9 108.1 %reduce-scatter.3.cloned.1.call-start = ((), (), s32[]{:S(2)}) async-start(), calls=%async_computation.3 | async-start | bytes 7864320 | tf_op jit(solution)/shard_map/reduce_scatter | solution.py:30
  58.1 57.9 %copy-start = (bf16[192,2048]{1,0:T(8,128)(2,1)S(1)}, bf16[192,2048]{1,0:T(8,128)(2,1)}, u32[]{:S(2)}) copy-start(bf16[192,2048]{1,0:T(8,128)(2,1)} %param.7) | copy-start | bytes 2359300
  58.2 90.2 %all-gather.7.cloned.1.call-start = ((), (), s32[]{:S(2)}) async-start(), calls=%async_computation.4 | async-start | bytes 3932160 | tf_op jit(solution)/shard_map/all_gather | solution.py:41
  119.7 67.1 %all-gather.9.cloned.1.call-start = ((), (), s32[]{:S(2)}) async-start(), calls=%async_computation.6 | async-start | bytes 1966080 | tf_op jit(solution)/shard_map/all_gather | solution.py:22
  120.3 95.4 %all-gather.11.cloned.1.call-start = ((), (), s32[]{:S(2)}) async-start(), calls=%async_computation.7 | async-start | bytes 3932160 | tf_op jit(solution)/shard_map/all_gather | solution.py:40
  120.9 157.4 %reduce-scatter.5.cloned.1.call-start = ((), (), s32[]{:S(2)}) async-start(), calls=%async_computation.5 | async-start | bytes 3932160 | tf_op jit(solution)/shard_map/reduce_scatter | solution.py:44
  156.7 30.2 %copy-start.1 = (bf16[768,2048]{1,0:T(8,128)(2,1)S(1)}, bf16[768,2048]{1,0:T(8,128)(2,1)}, u32[]{:S(2)}) copy-start(bf16[768,2048]{1,0:T(8,128)(2,1)} %all-gather.7.cloned.1.call-done) | copy-start | bytes 9437188
  194.0 21.7 %copy-start.2 = (bf16[768,1024]{1,0:T(8,128)(2,1)S(1)}, bf16[768,1024]{1,0:T(8,128)(2,1)}, u32[]{:S(2)}) copy-start(bf16[768,1024]{1,0:T(8,128)(2,1)} %all-gather.5.cloned.1.call-done) | copy-start | bytes 4718596
Sparse Core Ops, SparseCore 0:
  9.5 39.7 all-gather.4
  58.3 57.7 reduce-scatter.2
  119.9 28.4 all-gather.6
  149.8 37.0 all-gather.8
  188.3 27.3 all-gather.10
  217.9 60.3 reduce-scatter.4
where the time goes:
time: 287 us
  waiting for transfers between devices  226 us (79%)
  matrix products  31.8 us (11%)
  between operations  14.1 us (5%)
  local copies, waits for them, and re-layouts  9.45 us (3%)
  other arithmetic  5.61 us (2%)
    reduce_scatter x1, waiting for transfers between devices, per_device(): lax.psum_scatter(lax.dot_general(piece, down_weight, last_dims, preferred...  57.8 us
    reduce_scatter x1, waiting for transfers between devices, per_device(): lax.psum_scatter(lax.dot_general(piece, up_weight, last_dims, preferred_e...  55 us
    all_gather x1, waiting for transfers between devices, per_device(): lax.all_gather(cotangent, 'col', axis=0, tiled=True)  41.4 us
    all_gather x1, waiting for transfers between devices, per_device(): lax.all_gather(inputs, 'col', axis=0, tiled=True)  30.2 us
    all_gather x1, waiting for transfers between devices, per_device(): lax.all_gather(pre_grad, 'row', axis=0, tiled=True)  27.4 us
    all_gather x1, waiting for transfers between devices, per_device(): lax.all_gather(activation, 'row', axis=0, tiled=True)  12.3 us
    unnamed x7, local copies, waits for them, and re-layouts  9.45 us
    dot_general x1, matrix products, per_device(): lax.dot_general(piece, down_weight, last_dims, preferred_element_type=jnp...  8.82 us
  transfers between devices with their start and end apart: 6, of which 6 were waited for; matrix products, arithmetic and copies ran while one was open for 11% of the time, Pallas kernels for 0%

commit v1 on v0

v1 whole, which is shorter than its diff:
```python
import functools
import math

import jax
import jax.numpy as jnp
from jax import lax
from jax.experimental import pallas as pl
from jax.experimental.pallas import tpu as pltpu
from jax.sharding import PartitionSpec as P

F32, BF16 = jnp.float32, jnp.bfloat16
LAST = (((1,), (1,)), ((), ()))
FIRST = (((0,), (0,)), ((), ()))


def tanh_of(v):
    return jnp.tanh(0.7978845608 * (v + 0.044715 * v * v * v))


def gelu_value(values):
    v = values.astype(F32)
    return 0.5 * v * (1.0 + tanh_of(v))


def gelu_slope(values):
    v = values.astype(F32)
    t = tanh_of(v)
    return 0.5 * (1.0 + t) + 0.5 * v * (1.0 - t * t) * 0.7978845608 * (1.0 + 3.0 * 0.044715 * v * v)


def remote(src, dst, send, recv, where):
    return pltpu.make_async_remote_copy(
        src_ref=src, dst_ref=dst, send_sem=send, recv_sem=recv, device_id=where,
        device_id_type=pl.DeviceIdType.MESH,
    )


def block_at(c, t, nc):
    near = jnp.minimum(c, nc - 1 - c)
    step = -((t + 1) // 2) if t % 2 else t // 2
    return jnp.where(t <= 2 * near, c + step, jnp.where(2 * c < nc - 1, t, nc - 1 - t))


def kernel(
    nr, nc,
    x_ref, cot_ref, pre_ref, up_ref, down_ref,
    gi_ref, x_out, cot_out, act_out, pg_out,
    x_all, cot_all, pre_all, act_all, pg_all, up, down, part, h1_out, h1_in, h2_out, h2_in,
    gi_own, gi_out, gi_in,
    loc, cot_s, cot_r, x_s, x_r, pre_s, pre_r, h1_s, h1_r, h2_s, h2_r, pg_s, pg_r, gi_s, gi_r,
):
    r, c = lax.axis_index("row"), lax.axis_index("col")
    nx = nr // 2
    x, k = r // 2, r % 2
    mate = {"row": 2 * x + (1 - k)}
    tb, dr = gi_ref.shape
    ts, hc = pg_all.shape[1:]
    hb, db, eb = min(512, hc), min(512, dr), min(256, hc)
    peers = [(x + d) % nx for d in range(1, nx)]
    ends = []

    barrier = pltpu.get_barrier_semaphore()
    pl.semaphore_signal(barrier, inc=1, device_id=mate, device_id_type=pl.DeviceIdType.MESH)
    for p in peers:
        pl.semaphore_signal(barrier, inc=1, device_id={"row": 2 * p + k}, device_id_type=pl.DeviceIdType.MESH)
    for d in range(1, nc):
        pl.semaphore_signal(barrier, inc=1, device_id={"col": (c + d) % nc}, device_id_type=pl.DeviceIdType.MESH)
    local = [
        pltpu.make_async_copy(cot_ref, cot_all.at[c], loc.at[0]),
        pltpu.make_async_copy(down_ref, down, loc.at[1]),
        pltpu.make_async_copy(pre_ref, pre_all.at[pl.ds(r * nc, nc)], loc.at[2]),
        pltpu.make_async_copy(up_ref, up, loc.at[3]),
        pltpu.make_async_copy(x_ref, x_all.at[c], loc.at[4]),
    ]
    for copy in local:
        copy.start()
    pl.semaphore_wait(barrier, nx + nc - 1)

    def line(all_ref, send, recv, direction, j, source):
        return remote(source, all_ref.at[j], send.at[direction, j], recv.at[j],
                      {"col": c + 1 if direction == 0 else c - 1})

    def pass_on(all_ref, send, recv, own_ref, t):
        for direction, j in ((0, c - t), (1, c + t)):
            there = (j >= 0) & (j < nc)
            onward = (c + 1 < nc) if direction == 0 else (c >= 1)
            jj = jnp.clip(j, 0, nc - 1)
            if t > 0:
                @pl.when(there)
                def _():
                    line(all_ref, send, recv, direction, jj, all_ref.at[jj]).wait_recv()

            @pl.when(there & onward)
            def _():
                src = own_ref if t == 0 else all_ref.at[jj]
                line(all_ref, send, recv, direction, jj, src).start()

    def finish_line(all_ref, send, recv):
        for t in range(nc):
            for direction, j in ((0, c - t), (1, c + t)):
                onward = (c + 1 < nc) if direction == 0 else (c >= 1)
                jj = jnp.clip(j, 0, nc - 1)

                @pl.when((j >= 0) & (j < nc) & onward)
                def _():
                    line(all_ref, send, recv, direction, jj, all_ref.at[jj]).wait_send()

    def pre_copy(index, source_row, target_row, src=None):
        units = pre_all.at[pl.ds(source_row * nc, nc)]
        return remote(units if src is None else src, units, pre_s.at[index], pre_r.at[source_row],
                      {"row": target_row})

    def started(copy):
        copy.start()
        ends.append(copy)

    mate_row = 2 * x + (1 - k)
    pass_on(cot_all, cot_s, cot_r, cot_ref, 0)
    for i, p in enumerate(peers):
        started(pre_copy(1 + i, r, 2 * p + k, pre_ref))
    started(pre_copy(0, r, mate_row, pre_ref))

    def activate(row):
        steps = hc // eb

        def body(i, _):
            unit, at = row * nc + i // steps, pl.ds(pl.multiple_of((i % steps) * eb, eb), eb)
            act_all[unit, :, at] = gelu_value(pre_all[unit, :, at]).astype(BF16)
            return 0

        lax.fori_loop(0, nc * steps, body, 0)

    def s0(t):
        j = block_at(c, t, nc)
        if t == 0:
            local[0].wait()
            local[1].wait()
        block = cot_all[j]

        def body(i, _):
            at = pl.ds(pl.multiple_of(i * hb, hb), hb)
            got = lax.dot_general(block, down[at, :], LAST, preferred_element_type=F32)
            for s in range(nr):
                part[t, s, :, at] = got[s * ts : (s + 1) * ts]
            return 0

        lax.fori_loop(0, hc // hb, body, 0)
        for p in range(nx):
            h1_out[t, p] = part[t, 2 * p + (1 - k)].astype(BF16)
        started(remote(h1_out.at[t], h1_in.at[t], h1_s.at[t], h1_r.at[t], mate))

    def s1(t):
        remote(h1_out.at[t], h1_in.at[t], h1_s.at[t], h1_r.at[t], mate).wait_recv()
        for i, p in enumerate(peers):
            h2_out[t, i] = (part[t, 2 * p + k] + h1_in[t, p].astype(F32)).astype(BF16)
            started(remote(h2_out.at[t, i], h2_in.at[t, i], h2_s.at[t, i], h2_r.at[t, i],
                           {"row": 2 * p + k}))

    def pg_copy(t, index, source_row, target_row):
        unit = pg_all.at[block_at(c, t, nc) * nr + source_row]
        return remote(unit, unit, pg_s.at[t, index], pg_r.at[t, source_row], {"row": target_row})

    def s2(t):
        for i, p in enumerate(peers):
            remote(h2_out.at[t, i], h2_in.at[t, i], h2_s.at[t, i], h2_r.at[t, i],
                   {"row": 2 * p + k}).wait_recv()
        unit = block_at(c, t, nc) * nr + r

        def body(i, _):
            at = pl.ds(pl.multiple_of(i * eb, eb), eb)
            total = part[t, 2 * x + k, :, at] + h1_in[t, x, :, at].astype(F32)
            for i in range(nx - 1):
                total += h2_in[t, i, :, at].astype(F32)
            pg_all[unit, :, at] = (total * gelu_slope(pre_all[unit, :, at])).astype(BF16)
            return 0

        lax.fori_loop(0, hc // eb, body, 0)
        for i, p in enumerate(peers):
            started(pg_copy(t, 1 + i, r, 2 * p + k))
        started(pg_copy(t, 0, r, mate_row))

    def s3(t):
        for i, p in enumerate(peers):
            pg_copy(t, 0, 2 * p + k, mate_row).wait_recv()
            started(pg_copy(t, nx + i, 2 * p + k, mate_row))

    def gi_copy(j, source):
        return remote(gi_out.at[j], gi_in.at[source], gi_s.at[j], gi_r.at[source], {"col": j})

    def s4(t):
        j = block_at(c, t, nc)
        for p in range(nx):
            pg_copy(t, 0, 2 * p + (1 - k), mate_row).wait_recv()
        if t == 0:
            local[3].wait()
        units = pg_all[pl.ds(j * nr, nr)]

        def put(at, rows, got):
            if t == 0:
                gi_own[rows, at] = got
            else:
                gi_out[j, rows, at] = got.astype(BF16)

        def body(i, _):
            at = pl.ds(pl.multiple_of(i * db, db), db)
            if ts % 16 == 0:
                put(at, slice(None), lax.dot_general(
                    units.reshape(tb, hc), up[at, :], LAST, preferred_element_type=F32))
            else:
                got = [lax.dot_general(units[s], up[at, :], LAST, preferred_element_type=F32)
                       for s in range(nr)]
                put(at, slice(None), jnp.concatenate(got, axis=0))
            return 0

        lax.fori_loop(0, dr // db, body, 0)
        if t > 0:
            started(gi_copy(j, c))

    def out_copy(src, dst, index):
        copy = pltpu.make_async_copy(src, dst, loc.at[index])
        copy.start()
        outs.append(copy)

    outs = []
    for step in range(nc + 3):
        if 0 <= step - 2 < nc:
            s3(step - 2)
        if step < nc:
            if step > 0:
                pass_on(cot_all, cot_s, cot_r, cot_ref, step)
            s0(step)
            if step == 0:
                local[2].wait()
                activate(r)
            s1(step)
            if step == 0:
                pre_copy(0, mate_row, mate_row).wait_recv()
                activate(mate_row)
            if step == min(1, nc - 1):
                for i, p in enumerate(peers):
                    pre_copy(0, 2 * p + k, mate_row).wait_recv()
                    started(pre_copy(nx + i, 2 * p + k, mate_row))
                for p in peers:
                    pre_copy(0, 2 * p + (1 - k), mate_row).wait_recv()
            if step == nc - 1:
                out_copy(cot_all, cot_out, 5)
                local[4].wait()
                pass_on(x_all, x_s, x_r, x_ref, 0)
        if 0 <= step - 1 < nc:
            s2(step - 1)
        if 0 <= step - 2 < nc:
            s4(step - 2)
        if step == 2:
            for p in peers:
                activate(2 * p + k)
        if step == min(3, nc - 1):
            for p in peers:
                activate(2 * p + 1 - k)
            out_copy(act_all, act_out, 6)
        if step == nc + 1:
            out_copy(pg_all, pg_out, 7)
        if nc <= step < nc + nc - 1:
            pass_on(x_all, x_s, x_r, x_ref, step - nc + 1)
    for t in range(4, nc):
        pass_on(x_all, x_s, x_r, x_ref, t)
    out_copy(x_all, x_out, 8)
    total = gi_own[...]
    for d in range(1, nc):
        source = (c + d) % nc
        gi_copy(c, source).wait_recv()
        total += gi_in[source].astype(F32)
    gi_ref[...] = total.astype(BF16)
    for copy in ends:
        copy.wait_send()
    finish_line(cot_all, cot_s, cot_r)
    finish_line(x_all, x_s, x_r)
    for copy in outs:
        copy.wait()


def per_device(nr, nc, inputs, cotangent, preactivation, up_weight, down_weight):
    tb, dr = inputs.shape
    hc = up_weight.shape[1]
    ts, nx = tb // nr, nr // 2
    tokens = tb * nc
    dma = pltpu.SemaphoreType.DMA
    anywhere = pl.BlockSpec(memory_space=pl.ANY)
    shape = jax.ShapeDtypeStruct
    grad_input, x_all, cot_all, act_all, pg_all = pl.pallas_call(
        functools.partial(kernel, nr, nc),
        out_shape=(
            shape((tb, dr), BF16), shape((nc, tb, dr), BF16), shape((nc, tb, dr), BF16),
            shape((nc * nr, ts, hc), BF16), shape((nc * nr, ts, hc), BF16),
        ),
        in_specs=[anywhere] * 5,
        out_specs=(pl.BlockSpec(memory_space=pltpu.VMEM),) + (anywhere,) * 4,
        scratch_shapes=[
            pltpu.VMEM((nc, tb, dr), BF16), pltpu.VMEM((nc, tb, dr), BF16),
            pltpu.VMEM((nc * nr, ts, hc), BF16), pltpu.VMEM((nc * nr, ts, hc), BF16),
            pltpu.VMEM((nc * nr, ts, hc), BF16),
            pltpu.VMEM(up_weight.shape, BF16), pltpu.VMEM(down_weight.shape, BF16),
            pltpu.VMEM((nc, nr, ts, hc), F32),
            pltpu.VMEM((nc, nx, ts, hc), BF16), pltpu.VMEM((nc, nx, ts, hc), BF16),
            pltpu.VMEM((nc, nx - 1, ts, hc), BF16), pltpu.VMEM((nc, nx - 1, ts, hc), BF16),
            pltpu.VMEM((tb, dr), F32),
            pltpu.VMEM((nc, tb, dr), BF16), pltpu.VMEM((nc, tb, dr), BF16),
            dma((9,)), dma((2, nc)), dma((nc,)), dma((2, nc)), dma((nc,)),
            dma((2 * nx,)), dma((nr,)), dma((nc,)), dma((nc,)),
            dma((nc, nx - 1)), dma((nc, nx - 1)), dma((nc, 2 * nx)), dma((nc, nr)),
            dma((nc,)), dma((nc,)),
        ],
        compiler_params=pltpu.CompilerParams(
            collective_id=0, has_side_effects=True, vmem_limit_bytes=60 * 1024 * 1024
        ),
    )(inputs, cotangent, preactivation.reshape(nc, ts, hc), up_weight, down_weight)
    token_scale = 1.0 / math.sqrt(tokens)
    x_all, cot_all = x_all.reshape(tokens, dr), cot_all.reshape(tokens, dr)
    act_all, pg_all = act_all.reshape(tokens, hc), pg_all.reshape(tokens, hc)
    grad_up = lax.dot_general(x_all, pg_all, FIRST, preferred_element_type=F32) * token_scale
    grad_down = lax.dot_general(act_all, cot_all, FIRST, preferred_element_type=F32) * token_scale
    return (grad_input, grad_up, grad_down)


def solution(mesh):
    placed = (
        P(("groups", "col"), "row"),
        P(("groups", "col"), "row"),
        P(("groups", "row"), "col"),
        P("row", "col"),
        P("col", "row"),
    )
    return jax.shard_map(
        functools.partial(per_device, mesh.shape["row"], mesh.shape["col"]),
        mesh=mesh,
        in_specs=placed,
        out_specs=(
            P(("groups", "col"), "row"),
            P(("groups", "row"), "col"),
            P(("groups", "col"), "row"),
        ),
        check_vma=False,
    )
```

time: 287 us -> 135 us (0.47)
  waiting for transfers between devices: 226 us -> 0 us
  Pallas kernels: 0 us -> 116 us
  matrix products: 31.8 us -> 15.1 us
  between operations: 14.1 us -> 0.66 us
  local copies, waits for them, and re-layouts: 9.45 us -> 0.76 us
  other arithmetic: 5.61 us -> 0 us
    pallas_call x0 -> x1, Pallas kernels: none -> 116 us  [per_device(): pl.pallas_call(functools.partial(kernel, nr, nc), out_shape=(shape((tb, d...]
    reduce_scatter x2 -> x0, waiting for transfers between devices: 113 us -> none  [the longest x1 57.8 us: per_device(): lax.psum_scatter(lax.dot_general(piece, down_weight, last_dims, preferred...]
    all_gather x4 -> x0, waiting for transfers between devices: 111 us -> none  [the longest x1 41.4 us: per_device(): lax.all_gather(cotangent, 'col', axis=0, tiled=True)]
    dot_general x4 -> x2, matrix products: 31.8 us -> 15.1 us  [the longest x1 9.39 us: per_device(): lax.dot_general(x_all, pg_all, FIRST, preferred_element_type=F32)]
    unnamed x7, local copies, waits for them, and re-layouts: 9.45 us -> 0.76 us
    convert_element_type x2 -> x0, other arithmetic: 5.61 us -> none  [the longest x1 3.67 us: per_device(): activation = gelu_value.astype(jnp.bfloat16)]
  transfers between devices with their start and end apart: 6 -> 0, of which waited for: 6 -> 0; matrix products, arithmetic and copies ran while one was open for 11% -> 0% of each run, Pallas kernels for 0% -> 0%
where the time goes in v1:
time: 135 us; the launch traced here: 132 us
  Pallas kernels  116 us (86%)
  matrix products  15.1 us (11%)
    pallas_call x1, Pallas kernels, per_device(): pl.pallas_call(functools.partial(kernel, nr, nc), out_shape=(shape((tb, d...  116 us
    dot_general x1, matrix products, per_device(): lax.dot_general(x_all, pg_all, FIRST, preferred_element_type=F32)  9.39 us
    dot_general x1, matrix products, per_device(): lax.dot_general(act_all, cot_all, FIRST, preferred_element_type=F32)  5.75 us

profile of v1, /device:TPU:0, one launch (start us, length us, event | category | flops | bytes accessed | tf_op | source)
XLA Modules:
  0.0 132.4 jit_solution(10148145088841957467)
XLA Ops:
  0.6 115.9 %shard_map.76 = (bf16[192,1024]{1,0:T(8,128)(2,1)}, bf16[4,192,1024]{2,1,0:T(8,128)(2,1)}, bf16[4,192,1024]{2,1,0:T(8,128)(2,1)}, bf16[16,48,2048]{2,1,0:T(8,128)(2,1)}, bf16[16,48,2048]{2,1,0:T(8,128)(2,1)}) custom-call(bf16[192,1024]{1,0:T(8,128)(2,1)} %x_ref.1, bf16[192,1024]{1,0:T(8,128)(2,1)} %cot_ref.1, bf16[4,48,2048]{2,1,0:T(8,128)(2,1)} %bitcast.9, ...), custom_call_target="tpu_custom_call" | custom-call | tf_op jit(solution)/shard_map/pallas_call | solution.py:289
  116.5 0.0 copy-start.1
  116.5 0.0 copy-start.2
  116.5 9.4 %convolution_multiply_fusion.1 = f32[1024,2048]{1,0:T(8,128)} fusion(bf16[768,1024]{1,0:T(8,128)(2,1)} %bitcast.13, bf16[768,2048]{1,0:T(8,128)(2,1)} %bitcast.11), kind=kOutput, calls=%fused_computation.1 | convolution fusion | flops 3223322624 | bytes 13107200 | tf_op jit(solution)/shard_map/dot_general | solution.py:319
  125.9 0.0 copy-done.1
  125.9 0.0 copy-done.2
  125.9 0.0 copy-start
  125.9 5.8 %convolution_multiply_fusion = f32[2048,1024]{1,0:T(8,128)} fusion(bf16[768,2048]{1,0:T(8,128)(2,1)S(1)} %bitcast.10, bf16[768,1024]{1,0:T(8,128)(2,1)S(1)} %bitcast.12), kind=kOutput, calls=%fused_computation | convolution fusion | flops 3223322624 | bytes 13107200 | tf_op jit(solution)/shard_map/dot_general | solution.py:320
  131.7 0.0 copy-done
  131.7 0.7 copy.9
Async XLA Ops:
  116.5 9.4 %copy-start.1 = (bf16[16,48,2048]{2,1,0:T(8,128)(2,1)S(1)}, bf16[16,48,2048]{2,1,0:T(8,128)(2,1)}, u32[]{:S(2)}) copy-start(bf16[16,48,2048]{2,1,0:T(8,128)(2,1)} %get-tuple-element.11) | copy-start | bytes 9437188
  116.5 9.4 %copy-start.2 = (bf16[4,192,1024]{2,1,0:T(8,128)(2,1)S(1)}, bf16[4,192,1024]{2,1,0:T(8,128)(2,1)}, u32[]{:S(2)}) copy-start(bf16[4,192,1024]{2,1,0:T(8,128)(2,1)} %get-tuple-element.12) | copy-start | bytes 4718596
  125.9 5.8 %copy-start = (bf16[192,1024]{1,0:T(8,128)(2,1)S(1)}, bf16[192,1024]{1,0:T(8,128)(2,1)}, u32[]{:S(2)}) copy-start(bf16[192,1024]{1,0:T(8,128)(2,1)} %get-tuple-element.16) | copy-start | bytes 1179652

commit v2 on v1

--- a/solution.py
+++ b/solution.py
@@ -191,8 +191,6 @@
         j = block_at(c, t, nc)
         for p in range(nx):
             pg_copy(t, 0, 2 * p + (1 - k), mate_row).wait_recv()
-        if t == 0:
-            local[3].wait()
         units = pg_all[pl.ds(j * nr, nr)]
 
         def put(at, rows, got):
@@ -222,47 +220,80 @@
         outs.append(copy)
 
     outs = []
-    for step in range(nc + 3):
-        if 0 <= step - 2 < nc:
-            s3(step - 2)
-        if step < nc:
-            if step > 0:
-                pass_on(cot_all, cot_s, cot_r, cot_ref, step)
-            s0(step)
-            if step == 0:
-                local[2].wait()
-                activate(r)
-            s1(step)
-            if step == 0:
-                pre_copy(0, mate_row, mate_row).wait_recv()
-                activate(mate_row)
-            if step == min(1, nc - 1):
-                for i, p in enumerate(peers):
-                    pre_copy(0, 2 * p + k, mate_row).wait_recv()
-                    started(pre_copy(nx + i, 2 * p + k, mate_row))
-                for p in peers:
-                    pre_copy(0, 2 * p + (1 - k), mate_row).wait_recv()
-            if step == nc - 1:
-                out_copy(cot_all, cot_out, 5)
-                local[4].wait()
-                pass_on(x_all, x_s, x_r, x_ref, 0)
-        if 0 <= step - 1 < nc:
-            s2(step - 1)
-        if 0 <= step - 2 < nc:
-            s4(step - 2)
-        if step == 2:
+
+    def x_on(step):
+        for direction, far in ((0, c), (1, nc - 1 - c)):
+            t = step - far
+            j = c - t if direction == 0 else c + t
+            jj = jnp.clip(j, 0, nc - 1)
+            fits = (t >= 0) & (t <= far) & (far < nc - 1)
+
+            @pl.when(fits & (t > 0))
+            def _():
+                line(x_all, x_s, x_r, direction, jj, x_all.at[jj]).wait_recv()
+
+            @pl.when(fits)
+            def _():
+                line(x_all, x_s, x_r, direction, jj, x_all.at[jj]).start()
+
+    def x_rest():
+        for direction, far in ((0, c), (1, nc - 1 - c)):
+            for t in range(1, nc):
+                j = c - t if direction == 0 else c + t
+
+                @pl.when((far == nc - 1))
+                def _():
+                    jj = jnp.clip(j, 0, nc - 1)
+                    line(x_all, x_s, x_r, direction, jj, x_all.at[jj]).wait_recv()
+
+    local[4].wait()
+    for step in range(nc):
+        if step == 1:
+            local[3].wait()
+        if step > 0:
+            pass_on(cot_all, cot_s, cot_r, cot_ref, step)
+        x_on(step)
+        s0(step)
+        if step == 0:
+            local[2].wait()
+            activate(r)
+        s1(step)
+        if step == 0:
+            pre_copy(0, mate_row, mate_row).wait_recv()
+            activate(mate_row)
+        if step == min(2, nc - 1):
+            for i, p in enumerate(peers):
+                pre_copy(0, 2 * p + k, mate_row).wait_recv()
+                started(pre_copy(nx + i, 2 * p + k, mate_row))
             for p in peers:
-                activate(2 * p + k)
-        if step == min(3, nc - 1):
-            for p in peers:
-                activate(2 * p + 1 - k)
-            out_copy(act_all, act_out, 6)
-        if step == nc + 1:
-            out_copy(pg_all, pg_out, 7)
-        if nc <= step < nc + nc - 1:
-            pass_on(x_all, x_s, x_r, x_ref, step - nc + 1)
-    for t in range(4, nc):
-        pass_on(x_all, x_s, x_r, x_ref, t)
+                pre_copy(0, 2 * p + (1 - k), mate_row).wait_recv()
+        if step >= 2:
+            s2(step - 2)
+        if step >= 3:
+            s3(step - 3)
+    out_copy(cot_all, cot_out, 5)
+    onward = list(range(nc, 2 * nc - 3))
+    for at in onward[:1]:
+        x_on(at)
+    s2(nc - 2)
+    for p in peers:
+        activate(2 * p + k)
+    s3(nc - 3)
+    s2(nc - 1)
+    for t in range(1, nc - 2):
+        s4(t)
+    for at in onward[1:]:
+        x_on(at)
+    for p in peers:
+        activate(2 * p + 1 - k)
+    out_copy(act_all, act_out, 6)
+    s3(nc - 2)
+    s4(nc - 2)
+    s4(0)
+    s3(nc - 1)
+    s4(nc - 1)
+    out_copy(pg_all, pg_out, 7)
+    x_rest()
     out_copy(x_all, x_out, 8)
     total = gi_own[...]
     for d in range(1, nc):

time: 135 us -> 108 us (0.80); the launches traced: 132 us -> 108 us
  Pallas kernels: 116 us -> 91.6 us
    pallas_call x1, Pallas kernels: 116 us -> 91.6 us  [per_device(): pl.pallas_call(functools.partial(kernel, nr, nc), out_shape=(shape((tb, d...]
where the time goes in v2:
time: 108 us
  Pallas kernels  91.6 us (85%)
  matrix products  15.1 us (14%)
    pallas_call x1, Pallas kernels, per_device(): pl.pallas_call(functools.partial(kernel, nr, nc), out_shape=(shape((tb, d...  91.6 us
    dot_general x1, matrix products, per_device(): lax.dot_general(x_all, pg_all, FIRST, preferred_element_type=F32)  9.39 us
    dot_general x1, matrix products, per_device(): lax.dot_general(act_all, cot_all, FIRST, preferred_element_type=F32)  5.75 us

profile of v2, /device:TPU:0, one launch (start us, length us, event | category | flops | bytes accessed | tf_op | source)
XLA Modules:
  0.0 108.2 jit_solution(1138264859514151275)
XLA Ops:
  0.6 91.6 %shard_map.76 = (bf16[192,1024]{1,0:T(8,128)(2,1)}, bf16[4,192,1024]{2,1,0:T(8,128)(2,1)}, bf16[4,192,1024]{2,1,0:T(8,128)(2,1)}, bf16[16,48,2048]{2,1,0:T(8,128)(2,1)}, bf16[16,48,2048]{2,1,0:T(8,128)(2,1)}) custom-call(bf16[192,1024]{1,0:T(8,128)(2,1)} %x_ref.1, bf16[192,1024]{1,0:T(8,128)(2,1)} %cot_ref.1, bf16[4,48,2048]{2,1,0:T(8,128)(2,1)} %bitcast.9, ...), custom_call_target="tpu_custom_call" | custom-call | tf_op jit(solution)/shard_map/pallas_call | solution.py:320
  92.2 0.0 copy-start.1
  92.2 0.0 copy-start.2
  92.2 9.4 %convolution_multiply_fusion.1 = f32[1024,2048]{1,0:T(8,128)} fusion(bf16[768,1024]{1,0:T(8,128)(2,1)} %bitcast.13, bf16[768,2048]{1,0:T(8,128)(2,1)} %bitcast.11), kind=kOutput, calls=%fused_computation.1 | convolution fusion | flops 3223322624 | bytes 13107200 | tf_op jit(solution)/shard_map/dot_general | solution.py:350
  101.6 0.0 copy-done.1
  101.6 0.0 copy-done.2
  101.6 0.0 copy-start
  101.7 5.8 %convolution_multiply_fusion = f32[2048,1024]{1,0:T(8,128)} fusion(bf16[768,2048]{1,0:T(8,128)(2,1)S(1)} %bitcast.10, bf16[768,1024]{1,0:T(8,128)(2,1)S(1)} %bitcast.12), kind=kOutput, calls=%fused_computation | convolution fusion | flops 3223322624 | bytes 13107200 | tf_op jit(solution)/shard_map/dot_general | solution.py:351
  107.4 0.0 copy-done
  107.4 0.7 copy.9
Async XLA Ops:
  92.2 9.4 %copy-start.1 = (bf16[16,48,2048]{2,1,0:T(8,128)(2,1)S(1)}, bf16[16,48,2048]{2,1,0:T(8,128)(2,1)}, u32[]{:S(2)}) copy-start(bf16[16,48,2048]{2,1,0:T(8,128)(2,1)} %get-tuple-element.11) | copy-start | bytes 9437188
  92.2 9.4 %copy-start.2 = (bf16[4,192,1024]{2,1,0:T(8,128)(2,1)S(1)}, bf16[4,192,1024]{2,1,0:T(8,128)(2,1)}, u32[]{:S(2)}) copy-start(bf16[4,192,1024]{2,1,0:T(8,128)(2,1)} %get-tuple-element.12) | copy-start | bytes 4718596
  101.6 5.8 %copy-start = (bf16[192,1024]{1,0:T(8,128)(2,1)S(1)}, bf16[192,1024]{1,0:T(8,128)(2,1)}, u32[]{:S(2)}) copy-start(bf16[192,1024]{1,0:T(8,128)(2,1)} %get-tuple-element.16) | copy-start | bytes 1179652

commit v3 on v2

--- a/solution.py
+++ b/solution.py
@@ -47,7 +47,7 @@
     gi_ref, x_out, cot_out, act_out, pg_out,
     x_all, cot_all, pre_all, act_all, pg_all, up, down, part, h1_out, h1_in, h2_out, h2_in,
     gi_own, gi_out, gi_in,
-    loc, cot_s, cot_r, x_s, x_r, pre_s, pre_r, h1_s, h1_r, h2_s, h2_r, pg_s, pg_r, gi_s, gi_r,
+    loc, cot_s, cot_r, x_s, x_r, pre_s, pre_r, act_s, act_r, h1_s, h1_r, h2_s, h2_r, pg_s, pg_r, gi_s, gi_r,
 ):
     r, c = lax.axis_index("row"), lax.axis_index("col")
     nx = nr // 2
@@ -60,9 +60,8 @@
     ends = []
 
     barrier = pltpu.get_barrier_semaphore()
-    pl.semaphore_signal(barrier, inc=1, device_id=mate, device_id_type=pl.DeviceIdType.MESH)
-    for p in peers:
-        pl.semaphore_signal(barrier, inc=1, device_id={"row": 2 * p + k}, device_id_type=pl.DeviceIdType.MESH)
+    for d in range(1, nr):
+        pl.semaphore_signal(barrier, inc=1, device_id={"row": (r + d) % nr}, device_id_type=pl.DeviceIdType.MESH)
     for d in range(1, nc):
         pl.semaphore_signal(barrier, inc=1, device_id={"col": (c + d) % nc}, device_id_type=pl.DeviceIdType.MESH)
     local = [
@@ -74,7 +73,7 @@
     ]
     for copy in local:
         copy.start()
-    pl.semaphore_wait(barrier, nx + nc - 1)
+    pl.semaphore_wait(barrier, nr + nc - 2)
 
     def line(all_ref, send, recv, direction, j, source):
         return remote(source, all_ref.at[j], send.at[direction, j], recv.at[j],
@@ -105,10 +104,14 @@
                 def _():
                     line(all_ref, send, recv, direction, jj, all_ref.at[jj]).wait_send()
 
-    def pre_copy(index, source_row, target_row, src=None):
-        units = pre_all.at[pl.ds(source_row * nc, nc)]
-        return remote(units if src is None else src, units, pre_s.at[index], pre_r.at[source_row],
-                      {"row": target_row})
+    def act_copy(index, source_row, target_row):
+        units = act_all.at[pl.ds(source_row * nc, nc)]
+        return remote(units, units, act_s.at[index], act_r.at[source_row], {"row": target_row})
+
+    def pre_copy(i):
+        unit = r * nc + i
+        return remote(pre_ref.at[i], pre_all.at[unit], pre_s.at[i], pre_r.at[unit // nr],
+                      {"row": unit % nr}), unit % nr != r
 
     def started(copy):
         copy.start()
@@ -116,9 +119,9 @@
 
     mate_row = 2 * x + (1 - k)
     pass_on(cot_all, cot_s, cot_r, cot_ref, 0)
-    for i, p in enumerate(peers):
-        started(pre_copy(1 + i, r, 2 * p + k, pre_ref))
-    started(pre_copy(0, r, mate_row, pre_ref))
+    for i in range(nc):
+        copy, away = pre_copy(i)
+        pl.when(away)(copy.start)
 
     def activate(row):
         steps = hc // eb
@@ -164,7 +167,12 @@
         for i, p in enumerate(peers):
             remote(h2_out.at[t, i], h2_in.at[t, i], h2_s.at[t, i], h2_r.at[t, i],
                    {"row": 2 * p + k}).wait_recv()
-        unit = block_at(c, t, nc) * nr + r
+        j = block_at(c, t, nc)
+        unit = j * nr + r
+
+        @pl.when(unit // nc != r)
+        def _():
+            remote(pre_ref.at[0], pre_all.at[unit], pre_s.at[0], pre_r.at[j], mate).wait_recv()
 
         def body(i, _):
             at = pl.ds(pl.multiple_of(i * eb, eb), eb)
@@ -258,40 +266,33 @@
             local[2].wait()
             activate(r)
         s1(step)
-        if step == 0:
-            pre_copy(0, mate_row, mate_row).wait_recv()
-            activate(mate_row)
-        if step == min(2, nc - 1):
-            for i, p in enumerate(peers):
-                pre_copy(0, 2 * p + k, mate_row).wait_recv()
-                started(pre_copy(nx + i, 2 * p + k, mate_row))
-            for p in peers:
-                pre_copy(0, 2 * p + (1 - k), mate_row).wait_recv()
+        if step >= 1:
+            s2(step - 1)
         if step >= 2:
-            s2(step - 2)
-        if step >= 3:
-            s3(step - 3)
+            s3(step - 2)
     out_copy(cot_all, cot_out, 5)
     onward = list(range(nc, 2 * nc - 3))
     for at in onward[:1]:
         x_on(at)
-    s2(nc - 2)
-    for p in peers:
-        activate(2 * p + k)
-    s3(nc - 3)
-    s2(nc - 1)
     for t in range(1, nc - 2):
         s4(t)
+    s2(nc - 1)
+    for i, p in enumerate(peers):
+        started(act_copy(1 + i, r, 2 * p + k))
+    started(act_copy(0, r, mate_row))
+    s3(nc - 2)
+    s4(nc - 2)
     for at in onward[1:]:
         x_on(at)
-    for p in peers:
-        activate(2 * p + 1 - k)
-    out_copy(act_all, act_out, 6)
-    s3(nc - 2)
-    s4(nc - 2)
     s4(0)
     s3(nc - 1)
     s4(nc - 1)
+    for i, p in enumerate(peers):
+        act_copy(0, 2 * p + k, mate_row).wait_recv()
+        started(act_copy(nx + i, 2 * p + k, mate_row))
+    for p in range(nx):
+        act_copy(0, 2 * p + 1 - k, mate_row).wait_recv()
+    out_copy(act_all, act_out, 6)
     out_copy(pg_all, pg_out, 7)
     x_rest()
     out_copy(x_all, x_out, 8)
@@ -303,6 +304,9 @@
     gi_ref[...] = total.astype(BF16)
     for copy in ends:
         copy.wait_send()
+    for i in range(nc):
+        copy, away = pre_copy(i)
+        pl.when(away)(copy.wait_send)
     finish_line(cot_all, cot_s, cot_r)
     finish_line(x_all, x_s, x_r)
     for copy in outs:
@@ -336,7 +340,7 @@
             pltpu.VMEM((tb, dr), F32),
             pltpu.VMEM((nc, tb, dr), BF16), pltpu.VMEM((nc, tb, dr), BF16),
             dma((9,)), dma((2, nc)), dma((nc,)), dma((2, nc)), dma((nc,)),
-            dma((2 * nx,)), dma((nr,)), dma((nc,)), dma((nc,)),
+            dma((nc,)), dma((nc,)), dma((2 * nx,)), dma((nr,)), dma((nc,)), dma((nc,)),
             dma((nc, nx - 1)), dma((nc, nx - 1)), dma((nc, 2 * nx)), dma((nc, nr)),
             dma((nc,)), dma((nc,)),
         ],

time: 108 us -> 103 us (0.954)
  Pallas kernels: 91.6 us -> 86.5 us
    pallas_call x1, Pallas kernels: 91.6 us -> 86.5 us  [per_device(): pl.pallas_call(functools.partial(kernel, nr, nc), out_shape=(shape((tb, d...]
where the time goes in v3:
time: 103 us
  Pallas kernels  86.5 us (84%)
  matrix products  15.1 us (15%)
    pallas_call x1, Pallas kernels, per_device(): pl.pallas_call(functools.partial(kernel, nr, nc), out_shape=(shape((tb, d...  86.5 us
    dot_general x1, matrix products, per_device(): lax.dot_general(x_all, pg_all, FIRST, preferred_element_type=F32)  9.39 us
    dot_general x1, matrix products, per_device(): lax.dot_general(act_all, cot_all, FIRST, preferred_element_type=F32)  5.76 us

profile of v3, /device:TPU:0, one launch (start us, length us, event | category | flops | bytes accessed | tf_op | source)
XLA Modules:
  0.0 103.1 jit_solution(14007291172514567288)
XLA Ops:
  0.6 86.5 %shard_map.76 = (bf16[192,1024]{1,0:T(8,128)(2,1)}, bf16[4,192,1024]{2,1,0:T(8,128)(2,1)}, bf16[4,192,1024]{2,1,0:T(8,128)(2,1)}, bf16[16,48,2048]{2,1,0:T(8,128)(2,1)}, bf16[16,48,2048]{2,1,0:T(8,128)(2,1)}) custom-call(bf16[192,1024]{1,0:T(8,128)(2,1)} %x_ref.1, bf16[192,1024]{1,0:T(8,128)(2,1)} %cot_ref.1, bf16[4,48,2048]{2,1,0:T(8,128)(2,1)} %bitcast.9, ...), custom_call_target="tpu_custom_call" | custom-call | tf_op jit(solution)/shard_map/pallas_call | solution.py:324
  87.1 0.0 copy-start.1
  87.2 0.0 copy-start.2
  87.2 9.4 %convolution_multiply_fusion.1 = f32[1024,2048]{1,0:T(8,128)} fusion(bf16[768,1024]{1,0:T(8,128)(2,1)} %bitcast.13, bf16[768,2048]{1,0:T(8,128)(2,1)} %bitcast.11), kind=kOutput, calls=%fused_computation.1 | convolution fusion | flops 3223322624 | bytes 13107200 | tf_op jit(solution)/shard_map/dot_general | solution.py:354
  96.6 0.0 copy-done.1
  96.6 0.0 copy-done.2
  96.6 0.0 copy-start
  96.6 5.8 %convolution_multiply_fusion = f32[2048,1024]{1,0:T(8,128)} fusion(bf16[768,2048]{1,0:T(8,128)(2,1)S(1)} %bitcast.10, bf16[768,1024]{1,0:T(8,128)(2,1)S(1)} %bitcast.12), kind=kOutput, calls=%fused_computation | convolution fusion | flops 3223322624 | bytes 13107200 | tf_op jit(solution)/shard_map/dot_general | solution.py:355
  102.3 0.0 copy-done
  102.3 0.7 copy.9
Async XLA Ops:
  87.1 9.4 %copy-start.1 = (bf16[16,48,2048]{2,1,0:T(8,128)(2,1)S(1)}, bf16[16,48,2048]{2,1,0:T(8,128)(2,1)}, u32[]{:S(2)}) copy-start(bf16[16,48,2048]{2,1,0:T(8,128)(2,1)} %get-tuple-element.11) | copy-start | bytes 9437188
  87.2 9.4 %copy-start.2 = (bf16[4,192,1024]{2,1,0:T(8,128)(2,1)S(1)}, bf16[4,192,1024]{2,1,0:T(8,128)(2,1)}, u32[]{:S(2)}) copy-start(bf16[4,192,1024]{2,1,0:T(8,128)(2,1)} %get-tuple-element.12) | copy-start | bytes 4718596
  96.6 5.8 %copy-start = (bf16[192,1024]{1,0:T(8,128)(2,1)S(1)}, bf16[192,1024]{1,0:T(8,128)(2,1)}, u32[]{:S(2)}) copy-start(bf16[192,1024]{1,0:T(8,128)(2,1)} %get-tuple-element.16) | copy-start | bytes 1179652
